TPU v7x, 32 devices: a whole 2x2x4 slice. The times are simulated.
32 devices in a mesh: member: 2 (over y), tile: 4 (over z), sub: 4 (over x, core).
Axes of the slice: x: 2, y: 2, z: 4, core: 2. Of those that a mesh axis runs over, the one named last changes fastest.
Arguments:
- obs_forcing: bfloat16 [8, 4, 72, 8192], P('member', None, 'sub', 'tile'), parts along dimension 0, may hold values from -6 to 6
- transport_weights: bfloat16 [128, 64, 384], P('tile'), may hold values from -0.25 to 0.25
- block_offsets: int32 [128, 6], P('tile'), may hold values from -4 to 4
- edge_source: int32 [4, 4, 1], replicated, may hold values from 0 to 1
- edge_target: int32 [4, 4, 1], P('tile'), may hold values from 0 to 32, as said below
- edge_rotation: int32 [4, 4, 1], P('tile'), may hold values from 0 to 3
- edge_weight: float32 [4, 4, 1, 64], P('tile'), may hold values from -0.2 to 0.2
- mixing_rate: float32 [72, 8192], P('sub', 'tile'), may hold values from 0.02 to 0.3
- flux_profile: float32 [72], P('sub'), may hold values from 0.01 to 0.1
Outputs:
- adjoint_state: float32 [8, 72, 8192], P('member', 'sub', 'tile'), parts along dimension 0
- flux_grad: float32 [8, 8192], P('member', ('tile', 'sub')), parts along dimension 0
There are 2 independent parts, one for each index of `member`. A program takes and returns all parts, laid end to end along the dimension named above; an argument that names none is the same for every part. Nothing has to cross between parts.
Inputs may be any that keep to these rules, and one draw needn't show every extreme that they name: `edge_target`: 32 marks an empty slot; every other value is below 2. Receiver j has live slots only from the 3 or 4 tiles that border it across cube edges: j + 1 and j - 1 modulo 4, j + 4 // 2 modulo 4, and on some receivers j + 4 // 4 modulo 4; all other slots are empty.
All inputs are finite; a program needn't handle non-finite values.
Results may differ from a plain program's by a relative error of at most 0.015.
Values may be sent and summed in bfloat16 or wider, within the bound.
No kernel may reach another device: no remote copies, remote signals or barrier semaphores. Data moves between devices by JAX's collectives and lax.ppermute only.
A program may use at most 64 MiB of HBM per device.

v0:
```python
import jax
import jax.numpy as jnp
from jax import lax
from jax.sharding import PartitionSpec as P

LEV = 72
BLOCK = 64
HB = 4
STEPS = 16
NOBS = 4


def passed_along(array, axis, by):
    devices = lax.axis_size(axis)
    pairs = [(i, i + by) for i in range(devices) if 0 <= i + by < devices]
    return lax.ppermute(array, axis, pairs)


def extended_2(block, sides, width, periodic):
    for axis, dim in sides:
        count = lax.axis_size(axis)
        forward = [(i, i + 1) for i in range(count - 1)]
        if periodic:
            forward.append((count - 1, 0))
        backward = [(target, source) for source, target in forward]
        low = lax.ppermute(
            lax.slice_in_dim(block, block.shape[dim] - width, None, axis=dim), axis, forward
        )
        high = lax.ppermute(lax.slice_in_dim(block, 0, width, axis=dim), axis, backward)
        block = jnp.concatenate([low, block, high], axis=dim)
    return block


def rotation_table():
    position = jnp.arange(64, dtype=jnp.int32)
    grid_row = position // 8
    grid_col = position % 8
    return jnp.stack(
        [
            grid_row * 8 + grid_col,
            grid_col * 8 + (7 - grid_row),
            (7 - grid_row) * 8 + (7 - grid_col),
            (7 - grid_col) * 8 + grid_row,
        ]
    )


def body(
    obs_forcing,
    transport_weights,
    block_offsets,
    edge_source,
    edge_target,
    edge_rotation,
    edge_weight,
    mixing_rate,
    flux_profile,
):
    levels_dev = mixing_rate.shape[0]
    columns_dev = mixing_rate.shape[1]
    blocks_dev = columns_dev // BLOCK
    tracers = obs_forcing.shape[1]
    feature = tracers * levels_dev
    obs_every = STEPS // NOBS
    own_tile = lax.axis_index("tile")
    level_index = lax.axis_index("sub") * levels_dev + jnp.arange(levels_dev, dtype=jnp.int32)
    mixing = jnp.where((level_index < LEV - 1)[:, None], mixing_rate, jnp.float32(0.0))
    rate_below = passed_along(mixing[-1:], "sub", 1)
    mixing_ext = jnp.concatenate([rate_below, mixing], 0)
    nearby = jnp.arange(blocks_dev, dtype=jnp.int32)[:, None] + HB + block_offsets
    sources = lax.dynamic_index_in_dim(edge_source, own_tile, 0, keepdims=False).reshape(-1)
    target_flat = edge_target.reshape(-1)
    placement_matrix = (
        target_flat[:, None] == jnp.arange(blocks_dev, dtype=jnp.int32)[None, :]
    ).astype(jnp.float32)
    permuted_index = rotation_table()[edge_rotation.reshape(-1)]
    rotation_onehot = (
        jnp.arange(BLOCK, dtype=jnp.int32)[None, :, None] == permuted_index[:, None, :]
    ).astype(jnp.bfloat16)
    scale_rows = edge_weight.reshape(-1, BLOCK)
    span = transport_weights.shape[2]

    def transport(adjoint):
        rounded = adjoint.reshape(feature, columns_dev).astype(jnp.bfloat16)
        widened = extended_2(rounded, (("tile", 1),), HB * BLOCK, True)
        widened = widened.reshape(feature, blocks_dev + 2 * HB, BLOCK)
        picked = widened[:, nearby, :].reshape(feature, blocks_dev, span)
        moved_rows = jnp.einsum(
            "fbj,bdj->fbd", picked, transport_weights, preferred_element_type=jnp.float32
        )
        local_rows = rounded.reshape(feature, blocks_dev, BLOCK)
        received = lax.all_to_all(
            local_rows[:, sources, :], "tile", split_axis=1, concat_axis=1, tiled=True
        )
        rotated = jnp.einsum(
            "fsc,scp->fsp", received, rotation_onehot, preferred_element_type=jnp.float32
        )
        edge_term = jnp.einsum(
            "fsp,sb->fbp",
            rotated * scale_rows[None],
            placement_matrix,
            precision=lax.Precision.HIGHEST,
        )
        return (moved_rows + edge_term).reshape(tracers, levels_dev, columns_dev)

    def advance(step_count, state_pair):
        adjoint, gradient = state_pair
        step_index = STEPS - 1 - step_count
        obs_flag = (step_index % obs_every == obs_every - 1).astype(jnp.float32)
        forcing_now = lax.dynamic_index_in_dim(
            obs_forcing, step_index // obs_every, 0, keepdims=False
        ).astype(jnp.float32)
        adjoint = adjoint + obs_flag * forcing_now
        extended = extended_2(adjoint, (("sub", 1),), 1, False)
        flux_term = mixing_ext[None] * (extended[:, 1:] - extended[:, :-1])
        adjoint = adjoint + flux_term[:, 1:] - flux_term[:, :-1]
        adjoint = transport(adjoint)
        gradient = gradient + jnp.einsum(
            "tlc,l->tc", adjoint, flux_profile, precision=lax.Precision.HIGHEST
        )
        return (adjoint, gradient)

    initial = (
        jnp.zeros((tracers, levels_dev, columns_dev), jnp.float32),
        jnp.zeros((tracers, columns_dev), jnp.float32),
    )
    adjoint, gradient = lax.fori_loop(0, STEPS, advance, initial)
    flux_grad = lax.psum_scatter(
        gradient.astype(jnp.bfloat16), "sub", scatter_dimension=1, tiled=True
    ).astype(jnp.float32)
    return (adjoint, flux_grad)


def solution(mesh):
    return jax.shard_map(
        body,
        mesh=mesh,
        in_specs=(
            P("member", None, "sub", "tile"),
            P("tile", None, None),
            P("tile", None),
            P(),
            P("tile", None, None),
            P("tile", None, None),
            P("tile", None, None, None),
            P("sub", "tile"),
            P("sub"),
        ),
        out_specs=(P("member", "sub", "tile"), P("member", ("tile", "sub"))),
        check_vma=False,
    )
```

profile of v0, /device:TPU:0, one launch (start us, length us, event | category | flops | bytes accessed | tf_op | source)
XLA Modules:
  0.0 536.7 jit_solution(8276387351520853978)
XLA Ops:
  13.0 489.3 %while.18 = (s32[]{:T(128)}, f32[4,18,2048]{2,1,0:T(8,128)S(1)}, f32[4,2048]{1,0:T(4,128)S(1)}, bf16[4,4,18,2048]{3,1,2,0:T(4,128)(2,1)}, f32[19,2048]{1,0:T(8,1...) while((s32[]{:T(128)}, f32[4,18,2048]{2,1,0:T(8,128)S(1)}, ...), condition=%wide.region_1.2_spmd.clone, body=%wide.region_0.1_spmd.clone.sunk | while | flops 127284072 | bytes 21819072 | solution.py:127
  15.7 5.1 collective-permute-start.1
  28.2 5.1 all-to-all-start
  57.7 4.5 all-to-all-start
  77.7 4.0 collective-permute-start.1
  87.6 5.1 all-to-all-start
  118.1 5.1 all-to-all-start
  148.6 5.1 all-to-all-start
  169.2 4.0 collective-permute-start.1
  179.2 5.1 all-to-all-start
  209.7 5.1 all-to-all-start
  230.3 4.0 collective-permute-start.1
  240.2 5.1 all-to-all-start
  270.7 5.1 all-to-all-start
  301.3 5.1 all-to-all-start
  331.8 5.1 all-to-all-start
  352.4 4.0 collective-permute-start.1
  362.3 5.1 all-to-all-start
  392.9 5.1 all-to-all-start
  423.4 5.1 all-to-all-start
  453.9 5.1 all-to-all-start
  474.5 4.0 collective-permute-start.1
  484.4 5.1 all-to-all-start
  504.6 23.7 %reduce-scatter.4.cloned.1.call-done = bf16[512,4]{1,0:T(8,128)(2,1)} async-done(((bf16[2048,4]{1,0:T(8,128)(2,1)}), bf16[512,4]{1,0:T(8,128)(2,1)}) %reduce-scatter.4.cloned.1.call-update) | async-done | bytes 4112
  (661 shorter events, 388.7 us)
Async XLA Ops:
  7.2 521.1 %reduce-scatter.4.cloned.1.call-start = ((), (), s32[]{:S(2)}) async-start(), calls=%async_computation.2 | async-start | bytes 655360
  22.1 11.2 %collective-permute-start.2 = (bf16[72,256]{1,0:T(8,128)(2,1)S(1)}, bf16[72,256]{1,0:T(8,128)(2,1)S(1)}, u32[]{:S(2)}, u32[]{:S(2)}) collective-permute-start(bf16[72,256]{1,0:T(8,128)(2,1)S(1)} %get-tuple-element.506), channel_id=1, source_target_pairs={{4,0},{8,4},{12,8},{0,12},{5,1},{9,5},{13,9},{1,13},{6,2},{10,6},{... | collective-permute-start | bytes 110600 | tf_op jit(solution)/shard_map/while/body/eval_jaxpr/ppermute | solution.py:29
  28.2 10.9 %all-to-all-start = ((bf16[72,4,64]{0,2,1:T(8,128)(2,1)}), bf16[72,4,64]{0,2,1:T(8,128)(2,1)S(1)}, u32[]{:S(2)}, u32[]{:S(2)}) async-start(bf16[72,4,64]{0,2,1:T(8,128)(2,1)} %bitcast.82), calls=%async_computation | async-start | bytes 131072 | tf_op jit(solution)/shard_map/while/body/eval_jaxpr/all_to_all | solution.py:92
  57.7 10.3 %all-to-all-start = ((bf16[72,4,64]{0,2,1:T(8,128)(2,1)}), bf16[72,4,64]{0,2,1:T(8,128)(2,1)S(1)}, u32[]{:S(2)}, u32[]{:S(2)}) async-start(bf16[72,4,64]{0,2,1:T(8,128)(2,1)} %bitcast.82), calls=%async_computation | async-start | bytes 131072 | tf_op jit(solution)/shard_map/while/body/eval_jaxpr/all_to_all | solution.py:92
  87.6 10.9 %all-to-all-start = ((bf16[72,4,64]{0,2,1:T(8,128)(2,1)}), bf16[72,4,64]{0,2,1:T(8,128)(2,1)S(1)}, u32[]{:S(2)}, u32[]{:S(2)}) async-start(bf16[72,4,64]{0,2,1:T(8,128)(2,1)} %bitcast.82), calls=%async_computation | async-start | bytes 131072 | tf_op jit(solution)/shard_map/while/body/eval_jaxpr/all_to_all | solution.py:92
  118.1 10.9 %all-to-all-start = ((bf16[72,4,64]{0,2,1:T(8,128)(2,1)}), bf16[72,4,64]{0,2,1:T(8,128)(2,1)S(1)}, u32[]{:S(2)}, u32[]{:S(2)}) async-start(bf16[72,4,64]{0,2,1:T(8,128)(2,1)} %bitcast.82), calls=%async_computation | async-start | bytes 131072 | tf_op jit(solution)/shard_map/while/body/eval_jaxpr/all_to_all | solution.py:92
  144.0 9.7 %collective-permute-start.2 = (bf16[72,256]{1,0:T(8,128)(2,1)S(1)}, bf16[72,256]{1,0:T(8,128)(2,1)S(1)}, u32[]{:S(2)}, u32[]{:S(2)}) collective-permute-start(bf16[72,256]{1,0:T(8,128)(2,1)S(1)} %get-tuple-element.506), channel_id=1, source_target_pairs={{4,0},{8,4},{12,8},{0,12},{5,1},{9,5},{13,9},{1,13},{6,2},{10,6},{... | collective-permute-start | bytes 110600 | tf_op jit(solution)/shard_map/while/body/eval_jaxpr/ppermute | solution.py:29
  148.6 10.9 %all-to-all-start = ((bf16[72,4,64]{0,2,1:T(8,128)(2,1)}), bf16[72,4,64]{0,2,1:T(8,128)(2,1)S(1)}, u32[]{:S(2)}, u32[]{:S(2)}) async-start(bf16[72,4,64]{0,2,1:T(8,128)(2,1)} %bitcast.82), calls=%async_computation | async-start | bytes 131072 | tf_op jit(solution)/shard_map/while/body/eval_jaxpr/all_to_all | solution.py:92
  179.2 10.9 %all-to-all-start = ((bf16[72,4,64]{0,2,1:T(8,128)(2,1)}), bf16[72,4,64]{0,2,1:T(8,128)(2,1)S(1)}, u32[]{:S(2)}, u32[]{:S(2)}) async-start(bf16[72,4,64]{0,2,1:T(8,128)(2,1)} %bitcast.82), calls=%async_computation | async-start | bytes 131072 | tf_op jit(solution)/shard_map/while/body/eval_jaxpr/all_to_all | solution.py:92
  205.1 9.7 %collective-permute-start.2 = (bf16[72,256]{1,0:T(8,128)(2,1)S(1)}, bf16[72,256]{1,0:T(8,128)(2,1)S(1)}, u32[]{:S(2)}, u32[]{:S(2)}) collective-permute-start(bf16[72,256]{1,0:T(8,128)(2,1)S(1)} %get-tuple-element.506), channel_id=1, source_target_pairs={{4,0},{8,4},{12,8},{0,12},{5,1},{9,5},{13,9},{1,13},{6,2},{10,6},{... | collective-permute-start | bytes 110600 | tf_op jit(solution)/shard_map/while/body/eval_jaxpr/ppermute | solution.py:29
  209.7 10.9 %all-to-all-start = ((bf16[72,4,64]{0,2,1:T(8,128)(2,1)}), bf16[72,4,64]{0,2,1:T(8,128)(2,1)S(1)}, u32[]{:S(2)}, u32[]{:S(2)}) async-start(bf16[72,4,64]{0,2,1:T(8,128)(2,1)} %bitcast.82), calls=%async_computation | async-start | bytes 131072 | tf_op jit(solution)/shard_map/while/body/eval_jaxpr/all_to_all | solution.py:92
  240.2 10.9 %all-to-all-start = ((bf16[72,4,64]{0,2,1:T(8,128)(2,1)}), bf16[72,4,64]{0,2,1:T(8,128)(2,1)S(1)}, u32[]{:S(2)}, u32[]{:S(2)}) async-start(bf16[72,4,64]{0,2,1:T(8,128)(2,1)} %bitcast.82), calls=%async_computation | async-start | bytes 131072 | tf_op jit(solution)/shard_map/while/body/eval_jaxpr/all_to_all | solution.py:92
  266.1 9.7 %collective-permute-start.2 = (bf16[72,256]{1,0:T(8,128)(2,1)S(1)}, bf16[72,256]{1,0:T(8,128)(2,1)S(1)}, u32[]{:S(2)}, u32[]{:S(2)}) collective-permute-start(bf16[72,256]{1,0:T(8,128)(2,1)S(1)} %get-tuple-element.506), channel_id=1, source_target_pairs={{4,0},{8,4},{12,8},{0,12},{5,1},{9,5},{13,9},{1,13},{6,2},{10,6},{... | collective-permute-start | bytes 110600 | tf_op jit(solution)/shard_map/while/body/eval_jaxpr/ppermute | solution.py:29
  270.7 10.9 %all-to-all-start = ((bf16[72,4,64]{0,2,1:T(8,128)(2,1)}), bf16[72,4,64]{0,2,1:T(8,128)(2,1)S(1)}, u32[]{:S(2)}, u32[]{:S(2)}) async-start(bf16[72,4,64]{0,2,1:T(8,128)(2,1)} %bitcast.82), calls=%async_computation | async-start | bytes 131072 | tf_op jit(solution)/shard_map/while/body/eval_jaxpr/all_to_all | solution.py:92
  301.3 10.9 %all-to-all-start = ((bf16[72,4,64]{0,2,1:T(8,128)(2,1)}), bf16[72,4,64]{0,2,1:T(8,128)(2,1)S(1)}, u32[]{:S(2)}, u32[]{:S(2)}) async-start(bf16[72,4,64]{0,2,1:T(8,128)(2,1)} %bitcast.82), calls=%async_computation | async-start | bytes 131072 | tf_op jit(solution)/shard_map/while/body/eval_jaxpr/all_to_all | solution.py:92
  327.2 9.7 %collective-permute-start.2 = (bf16[72,256]{1,0:T(8,128)(2,1)S(1)}, bf16[72,256]{1,0:T(8,128)(2,1)S(1)}, u32[]{:S(2)}, u32[]{:S(2)}) collective-permute-start(bf16[72,256]{1,0:T(8,128)(2,1)S(1)} %get-tuple-element.506), channel_id=1, source_target_pairs={{4,0},{8,4},{12,8},{0,12},{5,1},{9,5},{13,9},{1,13},{6,2},{10,6},{... | collective-permute-start | bytes 110600 | tf_op jit(solution)/shard_map/while/body/eval_jaxpr/ppermute | solution.py:29
  331.8 10.9 %all-to-all-start = ((bf16[72,4,64]{0,2,1:T(8,128)(2,1)}), bf16[72,4,64]{0,2,1:T(8,128)(2,1)S(1)}, u32[]{:S(2)}, u32[]{:S(2)}) async-start(bf16[72,4,64]{0,2,1:T(8,128)(2,1)} %bitcast.82), calls=%async_computation | async-start | bytes 131072 | tf_op jit(solution)/shard_map/while/body/eval_jaxpr/all_to_all | solution.py:92
  362.3 10.9 %all-to-all-start = ((bf16[72,4,64]{0,2,1:T(8,128)(2,1)}), bf16[72,4,64]{0,2,1:T(8,128)(2,1)S(1)}, u32[]{:S(2)}, u32[]{:S(2)}) async-start(bf16[72,4,64]{0,2,1:T(8,128)(2,1)} %bitcast.82), calls=%async_computation | async-start | bytes 131072 | tf_op jit(solution)/shard_map/while/body/eval_jaxpr/all_to_all | solution.py:92
  388.2 9.7 %collective-permute-start.2 = (bf16[72,256]{1,0:T(8,128)(2,1)S(1)}, bf16[72,256]{1,0:T(8,128)(2,1)S(1)}, u32[]{:S(2)}, u32[]{:S(2)}) collective-permute-start(bf16[72,256]{1,0:T(8,128)(2,1)S(1)} %get-tuple-element.506), channel_id=1, source_target_pairs={{4,0},{8,4},{12,8},{0,12},{5,1},{9,5},{13,9},{1,13},{6,2},{10,6},{... | collective-permute-start | bytes 110600 | tf_op jit(solution)/shard_map/while/body/eval_jaxpr/ppermute | solution.py:29
  392.9 10.9 %all-to-all-start = ((bf16[72,4,64]{0,2,1:T(8,128)(2,1)}), bf16[72,4,64]{0,2,1:T(8,128)(2,1)S(1)}, u32[]{:S(2)}, u32[]{:S(2)}) async-start(bf16[72,4,64]{0,2,1:T(8,128)(2,1)} %bitcast.82), calls=%async_computation | async-start | bytes 131072 | tf_op jit(solution)/shard_map/while/body/eval_jaxpr/all_to_all | solution.py:92
  423.4 10.9 %all-to-all-start = ((bf16[72,4,64]{0,2,1:T(8,128)(2,1)}), bf16[72,4,64]{0,2,1:T(8,128)(2,1)S(1)}, u32[]{:S(2)}, u32[]{:S(2)}) async-start(bf16[72,4,64]{0,2,1:T(8,128)(2,1)} %bitcast.82), calls=%async_computation | async-start | bytes 131072 | tf_op jit(solution)/shard_map/while/body/eval_jaxpr/all_to_all | solution.py:92
  449.3 9.7 %collective-permute-start.2 = (bf16[72,256]{1,0:T(8,128)(2,1)S(1)}, bf16[72,256]{1,0:T(8,128)(2,1)S(1)}, u32[]{:S(2)}, u32[]{:S(2)}) collective-permute-start(bf16[72,256]{1,0:T(8,128)(2,1)S(1)} %get-tuple-element.506), channel_id=1, source_target_pairs={{4,0},{8,4},{12,8},{0,12},{5,1},{9,5},{13,9},{1,13},{6,2},{10,6},{... | collective-permute-start | bytes 110600 | tf_op jit(solution)/shard_map/while/body/eval_jaxpr/ppermute | solution.py:29
  453.9 10.9 %all-to-all-start = ((bf16[72,4,64]{0,2,1:T(8,128)(2,1)}), bf16[72,4,64]{0,2,1:T(8,128)(2,1)S(1)}, u32[]{:S(2)}, u32[]{:S(2)}) async-start(bf16[72,4,64]{0,2,1:T(8,128)(2,1)} %bitcast.82), calls=%async_computation | async-start | bytes 131072 | tf_op jit(solution)/shard_map/while/body/eval_jaxpr/all_to_all | solution.py:92
  484.4 10.9 %all-to-all-start = ((bf16[72,4,64]{0,2,1:T(8,128)(2,1)}), bf16[72,4,64]{0,2,1:T(8,128)(2,1)S(1)}, u32[]{:S(2)}, u32[]{:S(2)}) async-start(bf16[72,4,64]{0,2,1:T(8,128)(2,1)} %bitcast.82), calls=%async_computation | async-start | bytes 131072 | tf_op jit(solution)/shard_map/while/body/eval_jaxpr/all_to_all | solution.py:92
  (107 other events, 586.4 us)
Sparse Core Ops, SparseCore 0:
  503.5 24.6 reduce-scatter.3
where the time goes:
time: 540 us; the launch traced here: 537 us
  starting transfers between devices  204 us (38%)
  local copies, waits for them, and re-layouts  138 us (26%)
  matrix products  85.9 us (16%)
  waiting for transfers between devices  78.5 us (15%)
  between operations  14.2 us (3%)
  other arithmetic  12 us (2%)
    all_to_all x16, starting transfers between devices, transport(): lax.all_to_all(local_rows[:, sources, :], 'tile', split_axis=1, concat_ax...  80.7 us
    ppermute x32, starting transfers between devices, extended_2(): lax.ppermute(lax.slice_in_dim(block, block.shape[dim] - width, None, axis...  65.4 us
    dot_general x16, matrix products, transport(): jnp.einsum('fbj,bdj->fbd', picked, transport_weights, preferred_element_t...  55.5 us
    ppermute x32, starting transfers between devices, extended_2(): lax.ppermute(lax.slice_in_dim(block, 0, width, axis=dim), axis, backward)  55.4 us
    all_to_all x16, waiting for transfers between devices, transport(): lax.all_to_all(local_rows[:, sources, :], 'tile', split_axis=1, concat_ax...  43.7 us
    gather x16, local copies, waits for them, and re-layouts, transport(): picked = widened[:, nearby, :].reshape(feature, blocks_dev, span)  43.5 us
    unnamed x2, waiting for transfers between devices  23.7 us
    convert_element_type x48, local copies, waits for them, and re-layouts, transport(): rounded = adjoint.reshape(feature, columns_dev).astype(jnp.bfloat16)  22.2 us
  transfers between devices with their start and end apart: 82, of which 33 were waited for; matrix products, arithmetic and copies ran while one was open for 18% of the time, Pallas kernels for 0%

commit v1 on v0

--- a/solution.py
+++ b/solution.py
@@ -1,13 +1,20 @@
+import functools
+
 import jax
 import jax.numpy as jnp
 from jax import lax
+from jax.experimental import pallas as pl
+from jax.experimental.pallas import tpu as pltpu
 from jax.sharding import PartitionSpec as P
 
 LEV = 72
 BLOCK = 64
 HB = 4
+EB = 2
 STEPS = 16
 NOBS = 4
+LANES = 128
+GROUP = 4
 
 
 def passed_along(array, axis, by):
@@ -45,7 +52,7 @@
     )
 
 
-def body(
+def stepwise_body(
     obs_forcing,
     transport_weights,
     block_offsets,
@@ -131,9 +138,458 @@
     return (adjoint, flux_grad)
 
 
+def swap(array, axis, distance):
+    count = lax.axis_size(axis)
+    return lax.ppermute(array, axis, [(i, i ^ distance) for i in range(count)])
+
+
+def halo_depths():
+    every = STEPS // NOBS
+    return (STEPS, STEPS), tuple(every * (n + 1) for n in range(NOBS - 1))
+
+
+SMEM = pl.BlockSpec(memory_space=pltpu.SMEM)
+VMEM = pl.BlockSpec(memory_space=pltpu.VMEM)
+HBM = pl.BlockSpec(memory_space=pl.ANY)
+
+
+def cross(array, member_distance, sub_distance):
+    members, subs = lax.axis_size("member"), lax.axis_size("sub")
+    pairs = [
+        (i * subs + j, (i ^ member_distance) * subs + (j ^ sub_distance))
+        for i in range(members)
+        for j in range(subs)
+    ]
+    return lax.ppermute(array, ("member", "sub"), pairs)
+
+
+def pack_kernel(sizes, place, forcing, mixing, small, *messages):
+    tiles, levels, columns = sizes
+    first, later = messages[:tiles], messages[tiles:]
+    first_space = first[0].shape[0] - 2 * levels - 1
+    later_space = later[0].shape[0] - (NOBS - 1) * levels
+
+    def zeros(count):
+        return [jnp.zeros((count, LANES), jnp.float32)] if count else []
+
+    for d in range(tiles):
+        tracer = lax.bitwise_xor(place[0], d)
+
+        def one(c, _):
+            col = pl.ds(pl.multiple_of(c * LANES, LANES), LANES)
+
+            def plane(slot):
+                return forcing[slot, tracer, :, col].astype(jnp.float32)
+
+            lines = [mixing[:, col], plane(NOBS - 1), small[:, col]] + zeros(first_space)
+            first[d][:, col] = jnp.concatenate(lines, 0).astype(jnp.bfloat16)
+            lines = [plane(n) for n in range(NOBS - 1)] + zeros(later_space)
+            later[d][:, col] = jnp.concatenate(lines, 0).astype(jnp.bfloat16)
+            return 0
+
+        lax.fori_loop(0, columns // LANES, one, 0, unroll=4)
+
+
+def halo_kernel(levels, depths, *refs):
+    parts, (whole, upward, downward) = refs[:-3], refs[-3:]
+    space = upward.shape[1] - sum(depths)
+    fill = [jnp.zeros((space, LANES), jnp.float32)] if space else []
+    for d, part in enumerate(parts):
+
+        def one(c, _):
+            col = pl.ds(pl.multiple_of(c * LANES, LANES), LANES)
+            whole[d, :, col] = part[:, col]
+            lines = part[:, col].astype(jnp.float32)
+            top = [lines[(i + 1) * levels - n : (i + 1) * levels] for i, n in enumerate(depths)]
+            bottom = [lines[i * levels : i * levels + n] for i, n in enumerate(depths)]
+            upward[d, :, col] = jnp.concatenate(top + fill, 0).astype(jnp.bfloat16)
+            downward[d, :, col] = jnp.concatenate(bottom + fill, 0).astype(jnp.bfloat16)
+            return 0
+
+        lax.fori_loop(0, whole.shape[2] // LANES, one, 0, unroll=4)
+
+
+def halo_parts(levels, depths, parts):
+    count, (lines, columns) = len(parts), parts[0].shape
+    strip = (count, -(-sum(depths) // 8) * 8, columns)
+    return pl.pallas_call(
+        functools.partial(halo_kernel, levels, depths),
+        out_shape=tuple(
+            jax.ShapeDtypeStruct(shape, jnp.bfloat16)
+            for shape in ((count, lines, columns), strip, strip)
+        ),
+        in_specs=[VMEM] * count,
+        out_specs=(VMEM,) * 3,
+        compiler_params=pltpu.CompilerParams(vmem_limit_bytes=20000 * 1024),
+    )(*parts)
+
+
+def clear(bands, lo, hi):
+    def one(g, _):
+        for band in bands:
+            band[g] = jnp.zeros(band.shape[1:], band.dtype)
+        return 0
+
+    lax.fori_loop(lo, hi, one, 0, unroll=2)
+
+
+def add_group(bands, spot, offsets, g, slots, weights):
+    lane_low = lax.broadcasted_iota(jnp.int32, (BLOCK, LANES), 1) < BLOCK
+    for k in range(slots):
+        for side in range(2):
+            keep = lane_low if side == 0 else jnp.logical_not(lane_low)
+            for j, band in enumerate(bands):
+                at = side + 2 * j
+                w = offsets[(g * GROUP + at) * slots + k] + (at + HB)
+                part = weights(k * BLOCK, j * LANES)
+                part = jnp.where(keep, part, jnp.zeros((), jnp.bfloat16))
+                band[spot, w] = band[spot, w] + part
+
+
+def build_own_kernel(slots, offsets, weights, *bands):
+    clear(bands, 0, bands[0].shape[0])
+
+    def one(g, _):
+        rows = weights[pl.ds(pl.multiple_of(g * GROUP, GROUP), GROUP)]
+        turned = rows.reshape(GROUP * BLOCK, slots * BLOCK).T
+        add_group(
+            bands, g, offsets, g, slots,
+            lambda row, col: turned[row : row + BLOCK, col : col + LANES],
+        )
+        return 0
+
+    lax.fori_loop(0, bands[0].shape[0], one, 0)
+
+
+def band_shape(groups):
+    return (groups, GROUP + 2 * HB, BLOCK, LANES)
+
+
+def build_own(offsets, slots, weights):
+    shape = jax.ShapeDtypeStruct(band_shape(weights.shape[0] // GROUP), jnp.bfloat16)
+    return pl.pallas_call(
+        functools.partial(build_own_kernel, slots),
+        out_shape=(shape,) * (GROUP * BLOCK // LANES),
+        in_specs=[SMEM, VMEM],
+        out_specs=(VMEM,) * (GROUP * BLOCK // LANES),
+        compiler_params=pltpu.CompilerParams(vmem_limit_bytes=20000 * 1024),
+    )(offsets, weights)
+
+
+def transport_kernel(sizes, place, offsets, source, target, rotation, profile, *rest):
+    tiles, groups, rows, levels, own_lo, own_hi, window, tile_cols, per_pair, slots = sizes
+    first_depths, later_depths = halo_depths()
+    halves = GROUP * BLOCK // LANES
+    first, later, rest = rest[:3], rest[3:6], rest[6:]
+    own_bands, sent, rest = rest[:halves], rest[halves : halves + groups], rest[halves + groups :]
+    message, bands, rest = rest[0], rest[1 : 1 + halves], rest[1 + halves :]
+    held, even, odd, final, gradient, rate, edges, own_sems, sent_sems = rest
+    own_tile = place[0]
+    total_cols = tiles * tile_cols
+    wrap = HB * BLOCK // LANES
+
+    own_copies = [
+        pltpu.make_async_copy(own_bands[j], bands[j].at[pl.ds(0, groups)], own_sems.at[j])
+        for j in range(halves)
+    ]
+    sent_copies = [
+        pltpu.make_async_copy(sent[i], held.at[i], sent_sems.at[i]) for i in range(groups)
+    ]
+    for copy in sent_copies + own_copies:
+        copy.start()
+    clear(bands, groups, tiles * groups)
+
+    def field(refs, plane, depths, d, col):
+        low, own, high = (ref[d, :, col].astype(jnp.float32) for ref in refs)
+        depth, at = depths[plane], sum(depths[:plane])
+        edge = jnp.zeros((levels - depth, LANES), jnp.float32)
+        lines = [edge, low[at : at + depth], own[plane * levels : (plane + 1) * levels]]
+        lines += [high[at : at + depth], jnp.zeros((rows - 2 * levels - depth, LANES), jnp.float32)]
+        return jnp.concatenate([x for x in lines if x.shape[0]], 0)
+
+    def mixed(v, d, col):
+        flux = rate[d, :, col] * (pltpu.roll(v, rows - 1, 0) - v)
+        return (v + flux - pltpu.roll(flux, 1, 0)).astype(jnp.bfloat16)
+
+    def close_ring(dst):
+        for j in range(wrap):
+            dst[j] = dst[total_cols + j]
+            dst[total_cols + wrap + j] = dst[wrap + j]
+
+    column = lax.broadcasted_iota(jnp.int32, (BLOCK, LANES), 0)
+    lane = lax.broadcasted_iota(jnp.int32, (BLOCK, LANES), 1)
+    spot = lax.rem(lane, BLOCK)
+    side = 8
+    down, over = spot // side, lax.rem(spot, side)
+    turns = [
+        side * down + over,
+        side * over + (side - 1) - down,
+        side * (side - 1 - down) + (side - 1) - over,
+        side * (side - 1 - over) + down,
+    ]
+    half = lane // BLOCK
+
+    def start(d, _):
+        base = lax.bitwise_xor(d, own_tile) * tile_cols
+        for c in range(tile_cols):
+            col = pl.ds(c * LANES, LANES)
+            rate[d, :, col] = field(first, 0, first_depths, d, col)
+            even[base + wrap + c] = mixed(field(first, 1, first_depths, d, col), d, col)
+        for i in range(tiles):
+            for e in range(EB):
+                total = jnp.zeros((BLOCK, LANES), jnp.float32)
+                for n in range(per_pair):
+                    at = i * per_pair + n
+                    r = rotation[d, at]
+                    pick = jnp.where(r == 0, turns[0], turns[1])
+                    pick = jnp.where(r == 2, turns[2], pick)
+                    pick = jnp.where(r == 3, turns[3], pick)
+                    goes = jnp.where(source[d, at] == e, target[d, at], EB)
+                    weight = first[1][d, :, pl.ds((2 + at) * LANES, LANES)]
+                    weight = weight.astype(jnp.float32)[2 * levels : 2 * levels + 1]
+                    hit = jnp.logical_and(pick == column, half == goes)
+                    total = total + jnp.where(hit, weight, 0.0)
+                edges[d, pl.ds((i * EB + e) * BLOCK, BLOCK), :] = total.astype(jnp.bfloat16)
+        return 0
+
+    lax.fori_loop(0, tiles, start, 0)
+    for copy in sent_copies:
+        copy.wait()
+
+    def build(n, _):
+        d = lax.div(n, groups)
+        i = lax.rem(n, groups)
+        g = lax.bitwise_xor(place[1], i)
+        add_group(
+            bands, (d + 1) * groups + g, offsets, (d + 1) * groups + g, slots,
+            lambda row, col: held[i, d, pl.ds(row, BLOCK), pl.ds(col, LANES)],
+        )
+        return 0
+
+    lax.fori_loop(0, (tiles - 1) * groups, build, 0, unroll=2)
+    for copy in own_copies:
+        copy.wait()
+    close_ring(even)
+    gradient[...] = jnp.zeros(gradient.shape, jnp.float32)
+
+    def advance(src, dst, slot):
+        def one_tile(d, _):
+            base = lax.bitwise_xor(d, own_tile) * tile_cols
+            for g in range(groups):
+                near = jnp.concatenate(
+                    [src[base + 2 * g + j] for j in range(window // 2)], axis=1
+                )
+                matrix = jnp.concatenate(
+                    [b[d * groups + g].reshape(window * BLOCK, LANES) for b in bands], axis=1
+                )
+                moved = jnp.dot(near, matrix, preferred_element_type=jnp.float32)
+                for h in range(2):
+                    v = moved[:, h * LANES : (h + 1) * LANES]
+                    if g == 0 and h == 0:
+                        rim = jnp.concatenate(
+                            [src[wrap + i * tile_cols] for i in range(tiles)], axis=1
+                        )
+                        v = v + jnp.dot(rim, edges[d], preferred_element_type=jnp.float32)
+                    c = 2 * g + h
+                    col = pl.ds(c * LANES, LANES)
+                    own = v[own_lo:own_hi]
+                    weighted = own * profile[...]
+                    total = weighted[0:8]
+                    for r in range(8, own_hi - own_lo, 8):
+                        total = total + weighted[r : r + 8]
+                    gradient[d, :, col] = gradient[d, :, col] + total
+                    if slot is not None:
+                        final[d, :, col] = own
+                        v = v + slot(d, col)
+                    dst[base + wrap + c] = mixed(v, d, col)
+            return 0
+
+        lax.fori_loop(0, tiles, one_tile, 0)
+        close_ring(dst)
+
+    def cycle(n, _):
+        def next_forcing(d, col):
+            value = field(later, NOBS - 2, later_depths, d, col)
+            for slot in range(NOBS - 3, -1, -1):
+                value = jnp.where(n == NOBS - 2 - slot, field(later, slot, later_depths, d, col), value)
+            return value
+
+        for i in range(STEPS // NOBS):
+            src, dst = (even, odd) if i % 2 == 0 else (odd, even)
+            last = i == STEPS // NOBS - 1
+            advance(src, dst, next_forcing if last else None)
+        return 0
+
+    lax.fori_loop(0, NOBS, cycle, 0)
+
+    skip = levels - own_lo
+    space = message.shape[1] - levels - 1
+
+    def pack(d, _):
+        for c in range(tile_cols):
+            col = pl.ds(c * LANES, LANES)
+            lines = jnp.concatenate(
+                [
+                    final[d, skip : skip + levels, col],
+                    gradient[d, :, col].sum(0, keepdims=True),
+                    jnp.zeros((space, LANES), jnp.float32),
+                ],
+                0,
+            )
+            message[d, :, col] = lines.astype(jnp.bfloat16)
+        return 0
+
+    lax.fori_loop(0, tiles, pack, 0)
+
+
+def gathered_body(
+    obs_forcing,
+    transport_weights,
+    block_offsets,
+    edge_source,
+    edge_target,
+    edge_rotation,
+    edge_weight,
+    mixing_rate,
+    flux_profile,
+):
+    tiles, subs = (lax.axis_size(a) for a in ("tile", "sub"))
+    levels_dev, columns_dev = mixing_rate.shape
+    blocks_dev = columns_dev // BLOCK
+    groups = blocks_dev // GROUP
+    slots = block_offsets.shape[1]
+    span = slots * BLOCK
+    width = GROUP * BLOCK
+    per_pair = edge_target.shape[2]
+    tile_cols = columns_dev // LANES
+    window = GROUP + 2 * HB
+    own_lo = levels_dev // 8 * 8
+    own_hi = -(-2 * levels_dev // 8) * 8
+    rows = -(-3 * levels_dev // 8) * 8
+    m, t, s = (lax.axis_index(a) for a in ("member", "tile", "sub"))
+    place = jnp.stack([t, m * subs + s]).astype(jnp.int32)
+
+    turned = transport_weights.reshape(groups, GROUP, BLOCK, span)
+    share = lax.dynamic_index_in_dim(turned, m * subs + s, 0, keepdims=False)
+    share = share.transpose(2, 0, 1).reshape(span, width)
+    arrived = [swap(share, "tile", d) for d in range(1, tiles)]
+
+    n_off = blocks_dev * slots
+    n_edge = tiles * per_pair
+    weight = edge_weight.reshape(n_edge, BLOCK)
+    small = jnp.concatenate(
+        [
+            block_offsets.reshape(-1).astype(jnp.float32),
+            edge_target.reshape(-1).astype(jnp.float32),
+            edge_rotation.reshape(-1).astype(jnp.float32),
+        ]
+    )
+    small = jnp.pad(small, (0, 2 * LANES - small.shape[0]))
+    small = jnp.concatenate([small, jnp.concatenate([weight, weight], 1).reshape(-1)])
+    small = jnp.pad(small, (0, columns_dev - small.shape[0]))[None]
+    level_index = s * levels_dev + jnp.arange(levels_dev, dtype=jnp.int32)
+    mixing = jnp.where((level_index < LEV - 1)[:, None], mixing_rate, jnp.float32(0.0))
+
+    def lines(count):
+        return jax.ShapeDtypeStruct((-(-count // 8) * 8, columns_dev), jnp.bfloat16)
+
+    messages = pl.pallas_call(
+        functools.partial(pack_kernel, (tiles, levels_dev, columns_dev)),
+        out_shape=(lines(2 * levels_dev + 1),) * tiles
+        + (lines((NOBS - 1) * levels_dev),) * tiles,
+        in_specs=[SMEM] + [VMEM] * 3,
+        out_specs=(VMEM,) * (2 * tiles),
+        compiler_params=pltpu.CompilerParams(vmem_limit_bytes=20000 * 1024),
+    )(place, obs_forcing, mixing, small)
+    first, later = list(messages[:tiles]), list(messages[tiles:])
+    first, _ = lax.optimization_barrier((first, arrived[-1]))
+    first = [first[0]] + [swap(first[d], "tile", d) for d in range(1, tiles)]
+
+    here = jnp.stack(arrived)
+    beside = swap(here, "sub", 2)
+    across = swap(here, "member", 1)
+    corner = cross(here, 1, 2)
+    later, _ = lax.optimization_barrier((later, first))
+    later = [later[0]] + [swap(later[d], "tile", d) for d in range(1, tiles)]
+
+    def banded(own, depths):
+        own, upward, downward = halo_parts(levels_dev, depths, own)
+        low = lax.ppermute(upward, "sub", [(i, i + 1) for i in range(subs - 1)])
+        high = lax.ppermute(downward, "sub", [(i + 1, i) for i in range(subs - 1)])
+        return low, own, high
+
+    first_depths, later_depths = halo_depths()
+    small = jnp.stack([f[2 * levels_dev, : 2 * LANES] for f in first]).astype(jnp.int32)
+    first = banded(first, first_depths)
+    later = banded(later, later_depths)
+
+    offsets = small[:, :n_off]
+    target = small[:, n_off : n_off + n_edge]
+    rotation = small[:, n_off + n_edge : n_off + 2 * n_edge]
+    source = edge_source[:, t ^ jnp.arange(tiles)].transpose(1, 0, 2).reshape(tiles, n_edge)
+
+    own_bands = build_own(block_offsets.reshape(-1), slots, transport_weights)
+    sent = []
+    for part in (here, beside, across, corner):
+        sent += [part, swap(part, "sub", 1)]
+
+    profile = jnp.pad(
+        flux_profile, (levels_dev - own_lo, own_hi - 2 * levels_dev)
+    )
+    profile = jnp.broadcast_to(profile[:, None], (own_hi - own_lo, LANES))
+
+    sizes = (
+        tiles, groups, rows, levels_dev, own_lo, own_hi, window, tile_cols, per_pair, slots,
+    )
+    ring = (tiles * tile_cols + 2 * HB * BLOCK // LANES, rows, LANES)
+    message = pl.pallas_call(
+        functools.partial(transport_kernel, sizes),
+        out_shape=jax.ShapeDtypeStruct(
+            (tiles, -(-(levels_dev + 1) // 8) * 8, columns_dev), jnp.bfloat16
+        ),
+        in_specs=[SMEM] * 5 + [VMEM] * 7 + [HBM] * (len(own_bands) + len(sent)),
+        out_specs=VMEM,
+        scratch_shapes=[
+            *[pltpu.VMEM(band_shape(tiles * groups), jnp.bfloat16) for _ in own_bands],
+            pltpu.VMEM((groups, tiles - 1, span, width), jnp.bfloat16),
+            pltpu.VMEM(ring, jnp.bfloat16),
+            pltpu.VMEM(ring, jnp.bfloat16),
+            pltpu.VMEM((tiles, own_hi - own_lo, columns_dev), jnp.float32),
+            pltpu.VMEM((tiles, 8, columns_dev), jnp.float32),
+            pltpu.VMEM((tiles, rows, columns_dev), jnp.float32),
+            pltpu.VMEM((tiles, tiles * EB * BLOCK, EB * BLOCK), jnp.bfloat16),
+            pltpu.SemaphoreType.DMA((len(own_bands),)),
+            pltpu.SemaphoreType.DMA((len(sent),)),
+        ],
+        compiler_params=pltpu.CompilerParams(vmem_limit_bytes=44000 * 1024),
+    )(
+        place, offsets.reshape(-1), source, target, rotation, profile,
+        *first, *later, *own_bands, *sent,
+    )
+
+    parts = [message[0]] + [swap(message[d], "tile", d) for d in range(1, tiles)]
+    whole = jnp.stack(parts)[t ^ jnp.arange(tiles)]
+    adjoint = whole[:, :levels_dev].astype(jnp.float32)
+    partial_sum = whole[:, levels_dev].reshape(tiles, subs, columns_dev // subs)
+
+    def for_sub(d):
+        return lax.dynamic_index_in_dim(partial_sum, s ^ d, 1, keepdims=False)
+
+    flux_grad = for_sub(0).astype(jnp.float32)
+    for d in range(1, subs):
+        flux_grad = flux_grad + swap(for_sub(d), "sub", d).astype(jnp.float32)
+    return adjoint, flux_grad
+
+
+def gathers(mesh):
+    members, tiles, subs = (mesh.shape[a] for a in ("member", "tile", "sub"))
+    return (members, tiles, subs) == (2, 4, 4)
+
+
 def solution(mesh):
+    fits = gathers(mesh)
     return jax.shard_map(
-        body,
+        gathered_body if fits else stepwise_body,
         mesh=mesh,
         in_specs=(
             P("member", None, "sub", "tile"),

time: 540 us -> 158 us (0.29)
  starting transfers between devices: 204 us -> 42.6 us
  local copies, waits for them, and re-layouts: 138 us -> 15.7 us
  matrix products: 85.9 us -> 0 us
  Pallas kernels: 0 us -> 58.9 us
  waiting for transfers between devices: 78.5 us -> 37 us
  between operations: 14.2 us -> 0.97 us
  other arithmetic: 12 us -> 1.94 us
    dot_general x64 -> x0, matrix products: 85.9 us -> none  [the longest x16 55.5 us: transport(): jnp.einsum('fbj,bdj->fbd', picked, transport_weights, preferred_element_t...]
    all_to_all x16 -> x0, starting transfers between devices: 80.7 us -> none  [transport(): lax.all_to_all(local_rows[:, sources, :], 'tile', split_axis=1, concat_ax...]
    ppermute x65 -> x26, starting transfers between devices: 123 us -> 42.6 us  [the longest x21 30.6 us: swap(): return lax.ppermute(array, axis, [(i, i ^ distance) for i in range(count)])]
    gather x33 -> x2, local copies, waits for them, and re-layouts: 63.1 us -> 1.13 us  [the longest x1 0.57 us: gathered_body(): whole = jnp.stack(parts)[t ^ jnp.arange(tiles)]]
    pallas_call x0 -> x5, Pallas kernels: none -> 58.9 us  [the longest x1 52.8 us: gathered_body(): pl.pallas_call(functools.partial(transport_kernel, sizes), out_shape=jax....]
    all_to_all x16 -> x0, waiting for transfers between devices: 43.7 us -> none  [transport(): lax.all_to_all(local_rows[:, sources, :], 'tile', split_axis=1, concat_ax...]
    ppermute x65 -> x26, waiting for transfers between devices: 11.1 us -> 37 us  [the longest x21 37 us: swap(): return lax.ppermute(array, axis, [(i, i ^ distance) for i in range(count)])]
    unnamed x2 -> x0, waiting for transfers between devices: 23.7 us -> none
  transfers between devices with their start and end apart: 82 -> 26, of which waited for: 33 -> 10; matrix products, arithmetic and copies ran while one was open for 18% -> 6% of each run, Pallas kernels for 0% -> 4%
where the time goes in v1:
time: 158 us; the launch traced here: 157 us
  Pallas kernels  58.9 us (37%)
  starting transfers between devices  42.6 us (27%)
  waiting for transfers between devices  37 us (23%)
  local copies, waits for them, and re-layouts  15.7 us (10%)
  other arithmetic  1.94 us (1%)
    pallas_call x1, Pallas kernels, gathered_body(): pl.pallas_call(functools.partial(transport_kernel, sizes), out_shape=jax....  52.8 us
    ppermute x21, waiting for transfers between devices, swap(): return lax.ppermute(array, axis, [(i, i ^ distance) for i in range(count)])  37 us
    ppermute x21, starting transfers between devices, swap(): return lax.ppermute(array, axis, [(i, i ^ distance) for i in range(count)])  30.6 us
    unnamed x45, local copies, waits for them, and re-layouts  10.2 us
    ppermute x2, starting transfers between devices, banded(): low = lax.ppermute(upward, 'sub', [(i, i + 1) for i in range(subs - 1)])  7.01 us
  transfers between devices with their start and end apart: 26, of which 10 were waited for; matrix products, arithmetic and copies ran while one was open for 6% of the time, Pallas kernels for 4%

profile of v1, /device:TPU:0, one launch (start us, length us, event | category | flops | bytes accessed | tf_op | source)
XLA Modules:
  0.0 157.2 jit_solution(13216672502289835488)
XLA Ops:
  1.8 5.1 %collective-permute-start = (bf16[384,256]{1,0:T(8,128)(2,1)S(1)}, bf16[384,256]{1,0:T(8,128)(2,1)S(1)}, u32[]{:S(2)}, u32[]{:S(2)}) collective-permute-start(bf16[384,256]{1,0:T(8,128)(2,1)S(1)} %copy.18), channel_id=1, source_target_pairs={{0,12},{4,8},{8,4},{12,0},{1,13},{5,9},{9,5},{13,1},{2,14},{6,10},... | collective-permute-start | bytes 589832 | tf_op jit(solution)/shard_map/ppermute | solution.py:143
  9.3 2.0 %copy.17.forcing = bf16[4,4,18,2048]{3,2,1,0:T(8,128)(2,1)S(1)} copy(bf16[4,4,18,2048]{3,1,2,0:T(4,128)(2,1)} %param.9) | data formatting | bytes 2359296 | tf_op args[0]
  12.8 4.7 %collective-permute-start.1 = (bf16[40,2048]{1,0:T(8,128)(2,1)S(1)}, bf16[40,2048]{1,0:T(8,128)(2,1)S(1)}, u32[]{:S(2)}, u32[]{:S(2)}) collective-permute-start(bf16[40,2048]{1,0:T(8,128)(2,1)S(1)} %get-tuple-element.31), channel_id=1, source_target_pairs={{0,4},{4,0},{8,12},{12,8},{1,5},{5,1},{9,13},{13,9},{2,6},{6,2},{1... | collective-permute-start | bytes 491528 | tf_op jit(solution)/shard_map/ppermute | solution.py:143
  18.1 1.8 %collective-permute-start.3 = (bf16[40,2048]{1,0:T(8,128)(2,1)S(1)}, bf16[40,2048]{1,0:T(8,128)(2,1)S(1)}, u32[]{:S(2)}, u32[]{:S(2)}) collective-permute-start(bf16[40,2048]{1,0:T(8,128)(2,1)S(1)} %get-tuple-element.33), channel_id=1, source_target_pairs={{0,12},{4,8},{8,4},{12,0},{1,13},{5,9},{9,5},{13,1},{2,14},{6,10},... | collective-permute-start | bytes 491528 | tf_op jit(solution)/shard_map/ppermute | solution.py:143
  19.9 11.7 %collective-permute-done.12 = bf16[384,256]{1,0:T(8,128)(2,1)S(1)} collective-permute-done((bf16[384,256]{1,0:T(8,128)(2,1)S(1)}, bf16[384,256]{1,0:T(8,128)(2,1)S(1)}, u32[]{:S(2)}, u32[]{:S(2)}) %collective-permute-start.12) | collective-permute-done | bytes 196640 | tf_op jit(solution)/shard_map/ppermute | solution.py:143
  31.7 1.6 collective-permute-start.14
  33.2 1.9 %collective-permute-done.2.refs_2_ = bf16[40,2048]{1,0:T(8,128)(2,1)S(1)} collective-permute-done((bf16[40,2048]{1,0:T(8,128)(2,1)S(1)}, bf16[40,2048]{1,0:T(8,128)(2,1)S(1)}, u32[]{:S(2)}, u32[]{:S(2)}) %collective-permute-start.2) | collective-permute-done | bytes 163872 | tf_op jit(solution)/shard_map/ppermute | solution.py:143
  35.1 3.1 %collective-permute-start.6 = (bf16[56,2048]{1,0:T(8,128)(2,1)S(1)}, bf16[56,2048]{1,0:T(8,128)(2,1)S(1)}, u32[]{:S(2)}, u32[]{:S(2)}) collective-permute-start(bf16[56,2048]{1,0:T(8,128)(2,1)S(1)} %get-tuple-element.42), channel_id=1, source_target_pairs={{0,4},{4,0},{8,12},{12,8},{1,5},{5,1},{9,13},{13,9},{2,6},{6,2},{1... | collective-permute-start | bytes 688136 | tf_op jit(solution)/shard_map/ppermute | solution.py:143
  40.7 1.5 collective-permute-start.16
  42.2 4.6 %collective-permute-done.6.refs_1_ = bf16[56,2048]{1,0:T(8,128)(2,1)S(1)} collective-permute-done((bf16[56,2048]{1,0:T(8,128)(2,1)S(1)}, bf16[56,2048]{1,0:T(8,128)(2,1)S(1)}, u32[]{:S(2)}, u32[]{:S(2)}) %collective-permute-start.6) | collective-permute-done | bytes 229408 | tf_op jit(solution)/shard_map/ppermute | solution.py:143
  46.8 2.4 %collective-permute-start.18 = (bf16[3,384,256]{2,1,0:T(8,128)(2,1)S(1)}, bf16[3,384,256]{2,1,0:T(8,128)(2,1)}, u32[]{:S(2)}, u32[]{:S(2)}) collective-permute-start(bf16[3,384,256]{2,1,0:T(8,128)(2,1)S(1)} %pad_maximum_fusion.rest_8_), channel_id=1, source_target_pairs={{0,18},{1,19},{2,16},{3,17},{16,2},{17,3},{18,0},{19,1},{4,22},{5,... | collective-permute-start | bytes 1769480 | tf_op jit(solution)/shard_map/ppermute | solution.py:163
  49.3 8.2 %collective-permute-done.7.refs_2_ = bf16[56,2048]{1,0:T(8,128)(2,1)S(1)} collective-permute-done((bf16[56,2048]{1,0:T(8,128)(2,1)S(1)}, bf16[56,2048]{1,0:T(8,128)(2,1)S(1)}, u32[]{:S(2)}, u32[]{:S(2)}) %collective-permute-start.7) | collective-permute-done | bytes 229408 | tf_op jit(solution)/shard_map/ppermute | solution.py:143
  59.7 3.2 %collective-permute-start.4 = (bf16[4,32,2048]{2,1,0:T(8,128)(2,1)}, bf16[4,32,2048]{2,1,0:T(8,128)(2,1)}, u32[]{:S(2)}, u32[]{:S(2)}) collective-permute-start(bf16[4,32,2048]{2,1,0:T(8,128)(2,1)} %get-tuple-element.34), channel_id=1, source_target_pairs={{0,1},{1,2},{2,3},{4,5},{5,6},{6,7},{8,9},{9,10},{10,11},{12,13},{... | collective-permute-start | bytes 1572872 | tf_op jit(solution)/shard_map/ppermute | solution.py:517
  64.2 3.0 %collective-permute-done.16.rest_12_ = bf16[3,384,256]{2,1,0:T(8,128)(2,1)} collective-permute-done((bf16[3,384,256]{2,1,0:T(8,128)(2,1)S(1)}, bf16[3,384,256]{2,1,0:T(8,128)(2,1)}, u32[]{:S(2)}, u32[]{:S(2)}) %collective-permute-start.16) | collective-permute-done | bytes 589856 | tf_op jit(solution)/shard_map/ppermute | solution.py:143
  67.9 2.2 %shard_map.107 = (bf16[8,12,64,128]{3,2,1,0:T(8,128)(2,1)S(1)}, bf16[8,12,64,128]{3,2,1,0:T(8,128)(2,1)S(1)}) custom-call(s32[192]{0:T(256)S(1)} %reshape.54.offsets, bf16[32,64,384]{2,1,0:T(8,128)(2,1)S(1)} %copy-done), custom_call_target="tpu_custom_call" | custom-call | tf_op jit(solution)/shard_map/pallas_call | solution.py:270
  75.9 3.8 %collective-permute-start.9 = (bf16[4,24,2048]{2,1,0:T(8,128)(2,1)}, bf16[4,24,2048]{2,1,0:T(8,128)(2,1)}, u32[]{:S(2)}, u32[]{:S(2)}) collective-permute-start(bf16[4,24,2048]{2,1,0:T(8,128)(2,1)} %get-tuple-element.45), channel_id=1, source_target_pairs={{0,1},{1,2},{2,3},{4,5},{5,6},{6,7},{8,9},{9,10},{10,11},{12,13},{... | collective-permute-start | bytes 1179656 | tf_op jit(solution)/shard_map/ppermute | solution.py:517
  85.6 52.8 %shard_map.108 = bf16[4,24,2048]{2,1,0:T(8,128)(2,1)S(1)} custom-call(s32[2]{0:T(128)S(1)} %pad_add_fusion.place, s32[768]{0:T(1024)S(1)} %reshape.59.offsets, s32[4,4]{1,0:T(4,128)S(1)} %gather_fusion, s32[4,4]{1,0:T(4,128)S(1)} %get-tuple-element.63.target, s32[4,4]{1,0:T(4,128)S(1)} %get-tuple-element.62.rotation, ...), custom_call_target="tpu_custom_call" | custom-call | tf_op jit(solution)/shard_map/pallas_call | solution.py:545
  139.1 2.1 %collective-permute-start.21 = (bf16[24,2048]{1,0:T(8,128)(2,1)S(1)}, bf16[24,2048]{1,0:T(8,128)(2,1)S(1)}, u32[]{:S(2)}, u32[]{:S(2)}) collective-permute-start(bf16[24,2048]{1,0:T(8,128)(2,1)S(1)} %get-tuple-element.56), channel_id=1, source_target_pairs={{0,8},{4,12},{8,0},{12,4},{1,9},{5,13},{9,1},{13,5},{2,10},{6,14},... | collective-permute-start | bytes 294920 | tf_op jit(solution)/shard_map/ppermute | solution.py:143
  141.3 1.5 collective-permute-start.22
  143.0 2.4 %collective-permute-done.21 = bf16[24,2048]{1,0:T(8,128)(2,1)S(1)} collective-permute-done((bf16[24,2048]{1,0:T(8,128)(2,1)S(1)}, bf16[24,2048]{1,0:T(8,128)(2,1)S(1)}, u32[]{:S(2)}, u32[]{:S(2)}) %collective-permute-start.21) | collective-permute-done | bytes 98336 | tf_op jit(solution)/shard_map/ppermute | solution.py:143
  145.4 3.3 %collective-permute-done.22 = bf16[24,2048]{1,0:T(8,128)(2,1)S(1)} collective-permute-done((bf16[24,2048]{1,0:T(8,128)(2,1)S(1)}, bf16[24,2048]{1,0:T(8,128)(2,1)S(1)}, u32[]{:S(2)}, u32[]{:S(2)}) %collective-permute-start.22) | collective-permute-done | bytes 98336 | tf_op jit(solution)/shard_map/ppermute | solution.py:143
  149.6 2.0 %collective-permute-start.23 = (bf16[4,512]{1,0:T(4,128)(2,1)S(1)}, bf16[4,512]{1,0:T(4,128)(2,1)S(1)}, u32[]{:S(2)}, u32[]{:S(2)}) collective-permute-start(bf16[4,512]{1,0:T(4,128)(2,1)S(1)} %bitcast.57), channel_id=1, source_target_pairs={{0,1},{1,0},{2,3},{3,2},{4,5},{5,4},{6,7},{7,6},{8,9},{9,8},{10,11... | collective-permute-start | bytes 12296 | tf_op jit(solution)/shard_map/ppermute | solution.py:143
  151.5 2.0 %collective-permute-start.24 = (bf16[4,512]{1,0:T(4,128)(2,1)S(1)}, bf16[4,512]{1,0:T(4,128)(2,1)S(1)}, u32[]{:S(2)}, u32[]{:S(2)}) collective-permute-start(bf16[4,512]{1,0:T(4,128)(2,1)S(1)} %bitcast.58), channel_id=1, source_target_pairs={{0,2},{1,3},{2,0},{3,1},{4,6},{5,7},{6,4},{7,5},{8,10},{9,11},{10,... | collective-permute-start | bytes 12296 | tf_op jit(solution)/shard_map/ppermute | solution.py:143
  155.1 1.4 collective-permute-done.25
  (110 shorter events, 27.8 us)
Async XLA Ops:
  1.8 11.0 %collective-permute-start = (bf16[384,256]{1,0:T(8,128)(2,1)S(1)}, bf16[384,256]{1,0:T(8,128)(2,1)S(1)}, u32[]{:S(2)}, u32[]{:S(2)}) collective-permute-start(bf16[384,256]{1,0:T(8,128)(2,1)S(1)} %copy.18), channel_id=1, source_target_pairs={{0,12},{4,8},{8,4},{12,0},{1,13},{5,9},{9,5},{13,1},{2,14},{6,10},... | collective-permute-start | bytes 589832 | tf_op jit(solution)/shard_map/ppermute | solution.py:143
  6.9 13.0 %collective-permute-start.11 = (bf16[384,256]{1,0:T(8,128)(2,1)S(1)}, bf16[384,256]{1,0:T(8,128)(2,1)S(1)}, u32[]{:S(2)}, u32[]{:S(2)}) collective-permute-start(bf16[384,256]{1,0:T(8,128)(2,1)S(1)} %copy.18), channel_id=1, source_target_pairs={{0,4},{4,0},{8,12},{12,8},{1,5},{5,1},{9,13},{13,9},{2,6},{6,2},{1... | collective-permute-start | bytes 589832 | tf_op jit(solution)/shard_map/ppermute | solution.py:143
  6.9 24.7 %collective-permute-start.12 = (bf16[384,256]{1,0:T(8,128)(2,1)S(1)}, bf16[384,256]{1,0:T(8,128)(2,1)S(1)}, u32[]{:S(2)}, u32[]{:S(2)}) collective-permute-start(bf16[384,256]{1,0:T(8,128)(2,1)S(1)} %copy.18), channel_id=1, source_target_pairs={{0,8},{4,12},{8,0},{12,4},{1,9},{5,13},{9,1},{13,5},{2,10},{6,14},... | collective-permute-start | bytes 589832 | tf_op jit(solution)/shard_map/ppermute | solution.py:143
  12.8 20.4 %collective-permute-start.1 = (bf16[40,2048]{1,0:T(8,128)(2,1)S(1)}, bf16[40,2048]{1,0:T(8,128)(2,1)S(1)}, u32[]{:S(2)}, u32[]{:S(2)}) collective-permute-start(bf16[40,2048]{1,0:T(8,128)(2,1)S(1)} %get-tuple-element.31), channel_id=1, source_target_pairs={{0,4},{4,0},{8,12},{12,8},{1,5},{5,1},{9,13},{13,9},{2,6},{6,2},{1... | collective-permute-start | bytes 491528 | tf_op jit(solution)/shard_map/ppermute | solution.py:143
  17.5 17.6 %collective-permute-start.2 = (bf16[40,2048]{1,0:T(8,128)(2,1)S(1)}, bf16[40,2048]{1,0:T(8,128)(2,1)S(1)}, u32[]{:S(2)}, u32[]{:S(2)}) collective-permute-start(bf16[40,2048]{1,0:T(8,128)(2,1)S(1)} %get-tuple-element.32), channel_id=1, source_target_pairs={{0,8},{4,12},{8,0},{12,4},{1,9},{5,13},{9,1},{13,5},{2,10},{6,14},... | collective-permute-start | bytes 491528 | tf_op jit(solution)/shard_map/ppermute | solution.py:143
  18.1 17.0 %collective-permute-start.3 = (bf16[40,2048]{1,0:T(8,128)(2,1)S(1)}, bf16[40,2048]{1,0:T(8,128)(2,1)S(1)}, u32[]{:S(2)}, u32[]{:S(2)}) collective-permute-start(bf16[40,2048]{1,0:T(8,128)(2,1)S(1)} %get-tuple-element.33), channel_id=1, source_target_pairs={{0,12},{4,8},{8,4},{12,0},{1,13},{5,9},{9,5},{13,1},{2,14},{6,10},... | collective-permute-start | bytes 491528 | tf_op jit(solution)/shard_map/ppermute | solution.py:143
  31.7 31.3 %collective-permute-start.14 = (bf16[3,384,256]{2,1,0:T(8,128)(2,1)S(1)}, bf16[3,384,256]{2,1,0:T(8,128)(2,1)}, u32[]{:S(2)}, u32[]{:S(2)}) collective-permute-start(bf16[3,384,256]{2,1,0:T(8,128)(2,1)S(1)} %pad_maximum_fusion.rest_8_), channel_id=1, source_target_pairs={{0,2},{1,3},{2,0},{3,1},{4,6},{5,7},{6,4},{7,5},{8,10},{9,11},{10,... | collective-permute-start | bytes 1769480 | tf_op jit(solution)/shard_map/ppermute | solution.py:143
  35.1 11.7 %collective-permute-start.6 = (bf16[56,2048]{1,0:T(8,128)(2,1)S(1)}, bf16[56,2048]{1,0:T(8,128)(2,1)S(1)}, u32[]{:S(2)}, u32[]{:S(2)}) collective-permute-start(bf16[56,2048]{1,0:T(8,128)(2,1)S(1)} %get-tuple-element.42), channel_id=1, source_target_pairs={{0,4},{4,0},{8,12},{12,8},{1,5},{5,1},{9,13},{13,9},{2,6},{6,2},{1... | collective-permute-start | bytes 688136 | tf_op jit(solution)/shard_map/ppermute | solution.py:143
  38.2 19.2 %collective-permute-start.7 = (bf16[56,2048]{1,0:T(8,128)(2,1)S(1)}, bf16[56,2048]{1,0:T(8,128)(2,1)S(1)}, u32[]{:S(2)}, u32[]{:S(2)}) collective-permute-start(bf16[56,2048]{1,0:T(8,128)(2,1)S(1)} %get-tuple-element.43), channel_id=1, source_target_pairs={{0,8},{4,12},{8,0},{12,4},{1,9},{5,13},{9,1},{13,5},{2,10},{6,14},... | collective-permute-start | bytes 688136 | tf_op jit(solution)/shard_map/ppermute | solution.py:143
  39.3 20.4 %collective-permute-start.8 = (bf16[56,2048]{1,0:T(8,128)(2,1)S(1)}, bf16[56,2048]{1,0:T(8,128)(2,1)S(1)}, u32[]{:S(2)}, u32[]{:S(2)}) collective-permute-start(bf16[56,2048]{1,0:T(8,128)(2,1)S(1)} %get-tuple-element.44), channel_id=1, source_target_pairs={{0,12},{4,8},{8,4},{12,0},{1,13},{5,9},{9,5},{13,1},{2,14},{6,10},... | collective-permute-start | bytes 688136 | tf_op jit(solution)/shard_map/ppermute | solution.py:143
  40.7 26.6 %collective-permute-start.16 = (bf16[3,384,256]{2,1,0:T(8,128)(2,1)S(1)}, bf16[3,384,256]{2,1,0:T(8,128)(2,1)}, u32[]{:S(2)}, u32[]{:S(2)}) collective-permute-start(bf16[3,384,256]{2,1,0:T(8,128)(2,1)S(1)} %pad_maximum_fusion.rest_8_), channel_id=1, source_target_pairs={{0,16},{16,0},{1,17},{17,1},{2,18},{18,2},{3,19},{19,3},{4,20},{20... | collective-permute-start | bytes 1769480 | tf_op jit(solution)/shard_map/ppermute | solution.py:143
  46.8 20.4 %collective-permute-start.18 = (bf16[3,384,256]{2,1,0:T(8,128)(2,1)S(1)}, bf16[3,384,256]{2,1,0:T(8,128)(2,1)}, u32[]{:S(2)}, u32[]{:S(2)}) collective-permute-start(bf16[3,384,256]{2,1,0:T(8,128)(2,1)S(1)} %pad_maximum_fusion.rest_8_), channel_id=1, source_target_pairs={{0,18},{1,19},{2,16},{3,17},{16,2},{17,3},{18,0},{19,1},{4,22},{5,... | collective-permute-start | bytes 1769480 | tf_op jit(solution)/shard_map/ppermute | solution.py:163
  57.5 10.3 %collective-permute-start.13 = (bf16[3,384,256]{2,1,0:T(8,128)(2,1)S(1)}, bf16[3,384,256]{2,1,0:T(8,128)(2,1)S(1)}, u32[]{:S(2)}, u32[]{:S(2)}) collective-permute-start(bf16[3,384,256]{2,1,0:T(8,128)(2,1)S(1)} %pad_maximum_fusion.rest_8_), channel_id=1, source_target_pairs={{0,1},{1,0},{2,3},{3,2},{4,5},{5,4},{6,7},{7,6},{8,9},{9,8},{10,11... | collective-permute-start | bytes 1769480 | tf_op jit(solution)/shard_map/ppermute | solution.py:143
  59.7 14.9 %collective-permute-start.4 = (bf16[4,32,2048]{2,1,0:T(8,128)(2,1)}, bf16[4,32,2048]{2,1,0:T(8,128)(2,1)}, u32[]{:S(2)}, u32[]{:S(2)}) collective-permute-start(bf16[4,32,2048]{2,1,0:T(8,128)(2,1)} %get-tuple-element.34), channel_id=1, source_target_pairs={{0,1},{1,2},{2,3},{4,5},{5,6},{6,7},{8,9},{9,10},{10,11},{12,13},{... | collective-permute-start | bytes 1572872 | tf_op jit(solution)/shard_map/ppermute | solution.py:517
  62.9 13.0 %collective-permute-start.5 = (bf16[4,32,2048]{2,1,0:T(8,128)(2,1)}, bf16[4,32,2048]{2,1,0:T(8,128)(2,1)}, u32[]{:S(2)}, u32[]{:S(2)}) collective-permute-start(bf16[4,32,2048]{2,1,0:T(8,128)(2,1)} %get-tuple-element.36), channel_id=1, source_target_pairs={{1,0},{2,1},{3,2},{5,4},{6,5},{7,6},{9,8},{10,9},{11,10},{13,12},{... | collective-permute-start | bytes 1572872 | tf_op jit(solution)/shard_map/ppermute | solution.py:518
  67.3 16.0 %collective-permute-start.15 = (bf16[3,384,256]{2,1,0:T(8,128)(2,1)}, bf16[3,384,256]{2,1,0:T(8,128)(2,1)}, u32[]{:S(2)}, u32[]{:S(2)}) collective-permute-start(bf16[3,384,256]{2,1,0:T(8,128)(2,1)} %collective-permute-done.14.rest_10_), channel_id=1, source_target_pairs={{0,1},{1,0},{2,3},{3,2},{4,5},{5,4},{6,7},{7,6},{8,9},{9,8},{10,11... | collective-permute-start | bytes 1769480 | tf_op jit(solution)/shard_map/ppermute | solution.py:143
  67.3 16.0 %collective-permute-start.17 = (bf16[3,384,256]{2,1,0:T(8,128)(2,1)}, bf16[3,384,256]{2,1,0:T(8,128)(2,1)}, u32[]{:S(2)}, u32[]{:S(2)}) collective-permute-start(bf16[3,384,256]{2,1,0:T(8,128)(2,1)} %collective-permute-done.16.rest_12_), channel_id=1, source_target_pairs={{0,1},{1,0},{2,3},{3,2},{4,5},{5,4},{6,7},{7,6},{8,9},{9,8},{10,11... | collective-permute-start | bytes 1769480 | tf_op jit(solution)/shard_map/ppermute | solution.py:143
  67.8 15.5 %collective-permute-start.19 = (bf16[3,384,256]{2,1,0:T(8,128)(2,1)}, bf16[3,384,256]{2,1,0:T(8,128)(2,1)}, u32[]{:S(2)}, u32[]{:S(2)}) collective-permute-start(bf16[3,384,256]{2,1,0:T(8,128)(2,1)} %collective-permute-done.18.rest_14_), channel_id=1, source_target_pairs={{0,1},{1,0},{2,3},{3,2},{4,5},{5,4},{6,7},{7,6},{8,9},{9,8},{10,11... | collective-permute-start | bytes 1769480 | tf_op jit(solution)/shard_map/ppermute | solution.py:143
  74.6 8.6 %collective-permute-start.10 = (bf16[4,24,2048]{2,1,0:T(8,128)(2,1)}, bf16[4,24,2048]{2,1,0:T(8,128)(2,1)S(1)}, u32[]{:S(2)}, u32[]{:S(2)}) collective-permute-start(bf16[4,24,2048]{2,1,0:T(8,128)(2,1)} %get-tuple-element.47), channel_id=1, source_target_pairs={{1,0},{2,1},{3,2},{5,4},{6,5},{7,6},{9,8},{10,9},{11,10},{13,12},{... | collective-permute-start | bytes 1179656 | tf_op jit(solution)/shard_map/ppermute | solution.py:518
  75.9 7.4 %collective-permute-start.9 = (bf16[4,24,2048]{2,1,0:T(8,128)(2,1)}, bf16[4,24,2048]{2,1,0:T(8,128)(2,1)}, u32[]{:S(2)}, u32[]{:S(2)}) collective-permute-start(bf16[4,24,2048]{2,1,0:T(8,128)(2,1)} %get-tuple-element.45), channel_id=1, source_target_pairs={{0,1},{1,2},{2,3},{4,5},{5,6},{6,7},{8,9},{9,10},{10,11},{12,13},{... | collective-permute-start | bytes 1179656 | tf_op jit(solution)/shard_map/ppermute | solution.py:517
  138.4 4.7 %collective-permute-start.20 = (bf16[24,2048]{1,0:T(8,128)(2,1)S(1)}, bf16[24,2048]{1,0:T(8,128)(2,1)S(1)}, u32[]{:S(2)}, u32[]{:S(2)}) collective-permute-start(bf16[24,2048]{1,0:T(8,128)(2,1)S(1)} %get-tuple-element.57), channel_id=1, source_target_pairs={{0,4},{4,0},{8,12},{12,8},{1,5},{5,1},{9,13},{13,9},{2,6},{6,2},{1... | collective-permute-start | bytes 294920 | tf_op jit(solution)/shard_map/ppermute | solution.py:143
  139.1 6.3 %collective-permute-start.21 = (bf16[24,2048]{1,0:T(8,128)(2,1)S(1)}, bf16[24,2048]{1,0:T(8,128)(2,1)S(1)}, u32[]{:S(2)}, u32[]{:S(2)}) collective-permute-start(bf16[24,2048]{1,0:T(8,128)(2,1)S(1)} %get-tuple-element.56), channel_id=1, source_target_pairs={{0,8},{4,12},{8,0},{12,4},{1,9},{5,13},{9,1},{13,5},{2,10},{6,14},... | collective-permute-start | bytes 294920 | tf_op jit(solution)/shard_map/ppermute | solution.py:143
  141.3 7.5 %collective-permute-start.22 = (bf16[24,2048]{1,0:T(8,128)(2,1)S(1)}, bf16[24,2048]{1,0:T(8,128)(2,1)S(1)}, u32[]{:S(2)}, u32[]{:S(2)}) collective-permute-start(bf16[24,2048]{1,0:T(8,128)(2,1)S(1)} %get-tuple-element.55), channel_id=1, source_target_pairs={{0,12},{4,8},{8,4},{12,0},{1,13},{5,9},{9,5},{13,1},{2,14},{6,10},... | collective-permute-start | bytes 294920 | tf_op jit(solution)/shard_map/ppermute | solution.py:143
  149.6 5.4 %collective-permute-start.23 = (bf16[4,512]{1,0:T(4,128)(2,1)S(1)}, bf16[4,512]{1,0:T(4,128)(2,1)S(1)}, u32[]{:S(2)}, u32[]{:S(2)}) collective-permute-start(bf16[4,512]{1,0:T(4,128)(2,1)S(1)} %bitcast.57), channel_id=1, source_target_pairs={{0,1},{1,0},{2,3},{3,2},{4,5},{5,4},{6,7},{7,6},{8,9},{9,8},{10,11... | collective-permute-start | bytes 12296 | tf_op jit(solution)/shard_map/ppermute | solution.py:143
  (21 other events, 348.0 us)
